TPU v7x, 32 devices: a whole 2x2x4 slice. The times are simulated.
32 devices in a mesh: dp: 2 (over x), expert: 16 (over z, y, core).
Axes of the slice: x: 2, y: 2, z: 4, core: 2. Of those that a mesh axis runs over, the one named last changes fastest.
Arguments:
- saved_inputs: bfloat16 [1024, 3584], P('expert'), may hold values from -6 to 6
- output_grad: bfloat16 [1024, 3584], P('expert'), may hold values from -6 to 6
- routes: int32 [1024, 8], P('expert'), may hold values from 0 to 15, all different within a row; in each aligned block of 64 rows (0 to 63, 64 to 127, ...) at most 36 rows name the same one
- route_gates: bfloat16 [1024, 8], P('expert'), may hold values from 0.099609375 to 1
- expert_gate: bfloat16 [16, 3584, 1024], P('expert', None, 'dp'), may hold values from -0.09375 to 0.09375
- expert_up: bfloat16 [16, 3584, 1024], P('expert', None, 'dp'), may hold values from -0.09375 to 0.09375
- expert_down: bfloat16 [16, 1024, 3584], P('expert', 'dp'), may hold values from -0.1875 to 0.1875
- proj_basis: bfloat16 [16, 1024, 128], P('expert', 'dp'), may hold values from -0.1875 to 0.1875
Outputs:
- input_grad: bfloat16 [1024, 3584], P('expert', 'dp')
- projected: float32 [16, 3584, 3, 128], P('expert', 'dp')
Inputs may be any that keep to these rules, and one draw needn't show every extreme that they name: Within each aligned block of 64 tokens no expert is named by more than 36 routes, and in every draw some expert is named by exactly 36.
All inputs are finite; a program needn't handle non-finite values.
Results may differ from a plain program's by a relative error of at most 0.009.
Values may be sent and summed in bfloat16 or wider, within the bound.
A program may use at most 128 MiB of HBM per device.

v0:
```python
import jax
import jax.numpy as jnp
from jax import lax
from jax.sharding import PartitionSpec as P


def on_device(
    saved_inputs, output_grad, routes, route_gates, expert_gate, expert_up, expert_down, proj_basis
):
    token_count, model_width = saved_inputs.shape
    top_count = routes.shape[1]
    expert_count = lax.axis_size("expert")
    group_count = lax.axis_size("dp")
    capacity = token_count * top_count * 9 // (8 * expert_count)
    slot_count = expert_count * capacity
    column_width = model_width // group_count
    route_count = token_count * top_count
    flat_routes = routes.reshape(-1)
    one_hot = (flat_routes[:, None] == jnp.arange(expert_count, dtype=jnp.int32)[None, :]).astype(
        jnp.int32
    )
    earlier = jnp.sum((jnp.cumsum(one_hot, axis=0) - one_hot) * one_hot, axis=1)
    target_slot = flat_routes * capacity + earlier
    slot_owner = (
        jnp.full((slot_count,), route_count, jnp.int32)
        .at[target_slot]
        .set(jnp.arange(route_count, dtype=jnp.int32))
    )
    filled = slot_owner < route_count
    safe_route = jnp.minimum(slot_owner, route_count - 1)
    source_token = safe_route // top_count
    zero_half = jnp.zeros((), jnp.bfloat16)
    gate_slots = jnp.where(filled, route_gates.reshape(-1)[safe_route], zero_half).reshape(
        expert_count, capacity
    )
    token_map = (
        (source_token[None, :] == jnp.arange(token_count, dtype=jnp.int32)[:, None])
        & filled[None, :]
    ).astype(jnp.bfloat16)
    contract_first = (((0,), (0,)), ((), ()))

    def to_slots(source_rows):
        picked = lax.dot_general(
            token_map, source_rows, contract_first, preferred_element_type=jnp.float32
        ).astype(jnp.bfloat16)
        return picked.reshape(expert_count, capacity * source_rows.shape[1])

    recv_inputs, recv_grads, recv_gates = (
        lax.all_to_all(to_slots(saved_inputs), "expert", split_axis=0, concat_axis=0, tiled=True),
        lax.all_to_all(to_slots(output_grad), "expert", split_axis=0, concat_axis=0, tiled=True),
        lax.all_to_all(gate_slots, "expert", split_axis=0, concat_axis=0, tiled=True),
    )
    input_rows = recv_inputs.reshape(slot_count, model_width)
    grad_rows = recv_grads.reshape(slot_count, model_width)
    gain = recv_gates.reshape(slot_count, 1).astype(jnp.float32)
    gate_w = expert_gate[0]
    up_w = expert_up[0]
    down_w = expert_down[0]
    basis = proj_basis[0]
    rank_width = basis.shape[1]
    contract_last = (((1,), (1,)), ((), ()))
    pre_gate = jnp.dot(input_rows, gate_w, preferred_element_type=jnp.float32)
    pre_up = jnp.dot(input_rows, up_w, preferred_element_type=jnp.float32)
    grad_hidden = lax.dot_general(
        grad_rows, down_w, contract_last, preferred_element_type=jnp.float32
    )
    sigma = jax.nn.sigmoid(pre_gate)
    silu_val = pre_gate * sigma
    scaled = gain * grad_hidden
    grad_up = (scaled * silu_val).astype(jnp.bfloat16)
    grad_gate = (scaled * pre_up * sigma * (1.0 + pre_gate * (1.0 - sigma))).astype(jnp.bfloat16)
    hidden = (silu_val * pre_up).astype(jnp.bfloat16)
    part_rows = (
        lax.dot_general(grad_gate, gate_w, contract_last, preferred_element_type=jnp.float32)
        + lax.dot_general(grad_up, up_w, contract_last, preferred_element_type=jnp.float32)
    ).astype(jnp.bfloat16)
    coef_gate = jnp.dot(grad_gate, basis, preferred_element_type=jnp.float32).astype(jnp.bfloat16)
    coef_up = jnp.dot(grad_up, basis, preferred_element_type=jnp.float32).astype(jnp.bfloat16)
    coef_down = (gain * jnp.dot(hidden, basis, preferred_element_type=jnp.float32)).astype(
        jnp.bfloat16
    )
    coef_pair = jnp.concatenate([coef_gate, coef_up], axis=1)
    front = lax.dot_general(
        input_rows, coef_pair, contract_first, preferred_element_type=jnp.float32
    )
    rear = lax.dot_general(grad_rows, coef_down, contract_first, preferred_element_type=jnp.float32)
    summed_terms = lax.psum_scatter(
        jnp.concatenate([front, rear], axis=1).astype(jnp.bfloat16),
        "dp",
        scatter_dimension=0,
        tiled=True,
    ).astype(jnp.float32)
    projected = summed_terms.reshape(1, column_width, 3, rank_width)
    returned = lax.all_to_all(
        part_rows.reshape(expert_count, capacity * model_width),
        "expert",
        split_axis=0,
        concat_axis=0,
        tiled=True,
    )
    spread = jnp.dot(
        token_map, returned.reshape(slot_count, model_width), preferred_element_type=jnp.float32
    )
    token_grad = lax.psum_scatter(
        spread.astype(jnp.bfloat16), "dp", scatter_dimension=1, tiled=True
    )
    return (token_grad, projected)


def solution(mesh):
    placed = (
        P("expert", None),
        P("expert", None),
        P("expert", None),
        P("expert", None),
        P("expert", None, "dp"),
        P("expert", None, "dp"),
        P("expert", "dp", None),
        P("expert", "dp", None),
    )
    return jax.shard_map(
        on_device,
        mesh=mesh,
        in_specs=placed,
        out_specs=(P("expert", "dp"), P("expert", "dp", None, None)),
        check_vma=False,
    )
```

profile of v0, /device:TPU:0, one launch (start us, length us, event | category | flops | bytes accessed | tf_op | source)
XLA Modules:
  0.0 535.6 jit_solution(17826223306023978186)
XLA Ops:
  14.0 3.9 gather_fusion
  18.6 7.4 %all-to-all-start = ((bf16[16,1,36]{2,1,0:T(2,128)(2,1)}), bf16[16,1,36]{2,1,0:T(2,128)(2,1)S(1)}, u32[]{:S(2)}, u32[]{:S(2)}) async-start(bf16[16,1,36]{2,1,0:T(2,128)(2,1)} %all_to_all.32), calls=%async_computation | async-start | bytes 16384 | tf_op jit(solution)/shard_map/all_to_all | solution.py:51
  29.3 7.9 %all_to_all.34 = bf16[16,1,129024]{2,1,0:T(2,128)(2,1)} reshape(bf16[576,3584]{1,0:T(8,128)(2,1)} %convolution_convert_fusion) | data formatting | bytes 8257536 | tf_op jit(solution)/shard_map/all_to_all | solution.py:49
  37.8 26.8 %reduce.9 = bf16[16,129024]{1,0:T(8,128)(2,1)} reduce(bf16[16,1,129024]{2,1,0:T(2,128)(2,1)} %all_to_all.34, bf16[]{:T(256)} %broadcast.86), dimensions={1}, to_apply=%all_to_all.34.reduce_sub_computation | reduce | bytes 8257538 | tf_op jit(solution)/shard_map/all_to_all | solution.py:49
  64.6 6.6 %reshape.140 = bf16[16,2,64512]{2,1,0:T(2,128)(2,1)} reshape(bf16[16,129024]{1,0:T(8,128)(2,1)} %reduce.9) | data formatting | bytes 8257536
  71.2 6.7 %all-to-all-start.2 = ((bf16[16,2,64512]{2,1,0:T(2,128)(2,1)}), bf16[16,2,64512]{2,1,0:T(2,128)(2,1)}, u32[]{:S(2)}, u32[]{:S(2)}) async-start(bf16[16,2,64512]{2,1,0:T(2,128)(2,1)} %reshape.140), calls=%async_computation.2 | async-start | bytes 8257536 | tf_op jit(solution)/shard_map/all_to_all | solution.py:49
  81.1 7.9 %all_to_all.33 = bf16[16,1,129024]{2,1,0:T(2,128)(2,1)} reshape(bf16[576,3584]{1,0:T(8,128)(2,1)} %convolution_convert_fusion.1) | data formatting | bytes 8257536 | tf_op jit(solution)/shard_map/all_to_all | solution.py:50
  89.0 26.7 %reduce.10 = bf16[16,129024]{1,0:T(8,128)(2,1)} reduce(bf16[16,1,129024]{2,1,0:T(2,128)(2,1)} %all_to_all.33, bf16[]{:T(256)} %broadcast.86), dimensions={1}, to_apply=%all_to_all.33.reduce_sub_computation | reduce | bytes 8257538 | tf_op jit(solution)/shard_map/all_to_all | solution.py:50
  115.7 6.6 %reshape.142 = bf16[16,2,64512]{2,1,0:T(2,128)(2,1)} reshape(bf16[16,129024]{1,0:T(8,128)(2,1)} %reduce.10) | data formatting | bytes 8257536
  122.3 31.9 %all-to-all-done.2 = bf16[16,2,64512]{2,1,0:T(2,128)(2,1)} async-done(((bf16[16,2,64512]{2,1,0:T(2,128)(2,1)}), bf16[16,2,64512]{2,1,0:T(2,128)(2,1)}, u32[]{:S(2)}, u32[]{:S(2)}) %all-to-all-start.2) | async-done | bytes 4128800 | tf_op jit(solution)/shard_map/all_to_all | solution.py:49
  154.2 19.6 %all-to-all-start.1 = ((bf16[16,2,64512]{2,1,0:T(2,128)(2,1)}), bf16[16,2,64512]{2,1,0:T(2,128)(2,1)}, u32[]{:S(2)}, u32[]{:S(2)}) async-start(bf16[16,2,64512]{2,1,0:T(2,128)(2,1)} %reshape.142), calls=%async_computation.1 | async-start | bytes 8257536 | tf_op jit(solution)/shard_map/all_to_all | solution.py:50
  174.0 12.2 %reshape.141 = bf16[16,1,129024]{2,1,0:T(2,128)(2,1)} reshape(bf16[16,2,64512]{2,1,0:T(2,128)(2,1)} %all-to-all-done.2) | data formatting | bytes 8257536
  186.1 26.1 %reduce.3 = bf16[16,129024]{1,0:T(8,128)(2,1)} reduce(bf16[16,1,129024]{2,1,0:T(2,128)(2,1)} %reshape.141, bf16[]{:T(256)} %constant.41), dimensions={1}, to_apply=%all_to_all.29.reduce_sub_computation | reduce | bytes 8257538 | tf_op jit(solution)/shard_map/all_to_all | solution.py:49
  212.2 9.0 %reshape.103 = bf16[576,3584]{1,0:T(8,128)(2,1)} reshape(bf16[16,129024]{1,0:T(8,128)(2,1)} %reduce.3) | data formatting | bytes 8257536 | tf_op jit(solution)/shard_map/reshape | solution.py:53
  221.3 5.7 %fusion.2 = f32[576,512]{1,0:T(8,128)S(1)} fusion(bf16[576,3584]{1,0:T(8,128)(2,1)} %reshape.103, bf16[1,3584,512]{2,1,0:T(8,128)(2,1)} %param.12), kind=kOutput, calls=%fused_computation.10 | convolution fusion | flops 2113929216 | bytes 8978432 | tf_op jit(solution)/shard_map/dot_general | solution.py:62
  230.3 19.9 %all-to-all-done.1 = bf16[16,2,64512]{2,1,0:T(2,128)(2,1)} async-done(((bf16[16,2,64512]{2,1,0:T(2,128)(2,1)}), bf16[16,2,64512]{2,1,0:T(2,128)(2,1)}, u32[]{:S(2)}, u32[]{:S(2)}) %all-to-all-start.1) | async-done | bytes 4128800 | tf_op jit(solution)/shard_map/all_to_all | solution.py:50
  250.2 12.2 %reshape.143 = bf16[16,1,129024]{2,1,0:T(2,128)(2,1)} reshape(bf16[16,2,64512]{2,1,0:T(2,128)(2,1)} %all-to-all-done.1) | data formatting | bytes 8257536
  262.4 26.1 %reduce.2 = bf16[16,129024]{1,0:T(8,128)(2,1)} reduce(bf16[16,1,129024]{2,1,0:T(2,128)(2,1)} %reshape.143, bf16[]{:T(256)} %constant.41), dimensions={1}, to_apply=%all_to_all.27.reduce_sub_computation | reduce | bytes 8257538 | tf_op jit(solution)/shard_map/all_to_all | solution.py:50
  288.5 9.3 %reshape.102 = bf16[576,3584]{1,0:T(8,128)(2,1)} reshape(bf16[16,129024]{1,0:T(8,128)(2,1)} %reduce.2) | data formatting | bytes 8257536 | tf_op jit(solution)/shard_map/reshape | solution.py:54
  297.7 6.4 %multiply_convert_fusion.1 = (bf16[576,512]{1,0:T(8,128)(2,1)S(1)}, bf16[576,512]{1,0:T(8,128)(2,1)S(1)}) fusion(f32[576,512]{1,0:T(8,128)S(1)} %fusion.2, f32[576,512]{1,0:T(8,128)} %fusion.5, bf16[576,3584]{1,0:T(8,128)(2,1)} %reshape.102, bf16[1,512,3584]{2,1,0:T(8,128)(2,1)} %param.14, f32[576]{0:T(1024)S(1)} %reshape.107), kind=kOutput, calls=%fused_computation.20 | convolution fusion | flops 2118057984 | bytes 11340032 | tf_op jit(solution)/shard_map/dot_general | solution.py:64
  306.5 4.4 add_convert_fusion
  310.9 7.9 %all_to_all.35 = bf16[16,1,129024]{2,1,0:T(2,128)(2,1)} reshape(bf16[576,3584]{1,0:T(8,128)(2,1)} %add_convert_fusion) | data formatting | bytes 8257536 | tf_op jit(solution)/shard_map/all_to_all | solution.py:94
  318.8 26.8 %reduce.11 = bf16[16,129024]{1,0:T(8,128)(2,1)} reduce(bf16[16,1,129024]{2,1,0:T(2,128)(2,1)} %all_to_all.35, bf16[]{:T(256)} %broadcast.86), dimensions={1}, to_apply=%all_to_all.35.reduce_sub_computation | reduce | bytes 8257538 | tf_op jit(solution)/shard_map/all_to_all | solution.py:94
  345.6 6.8 %reshape.144 = bf16[16,2,64512]{2,1,0:T(2,128)(2,1)} reshape(bf16[16,129024]{1,0:T(8,128)(2,1)} %reduce.11) | data formatting | bytes 8257536
  352.4 19.5 %all-to-all-start.3 = ((bf16[16,2,64512]{2,1,0:T(2,128)(2,1)}), bf16[16,2,64512]{2,1,0:T(2,128)(2,1)}, u32[]{:S(2)}, u32[]{:S(2)}) async-start(bf16[16,2,64512]{2,1,0:T(2,128)(2,1)} %reshape.144), calls=%async_computation.3 | async-start | bytes 8257536 | tf_op jit(solution)/shard_map/all_to_all | solution.py:94
  376.4 4.3 convolution_convert_fusion.3
  382.5 65.8 %all-to-all-done.3 = bf16[16,2,64512]{2,1,0:T(2,128)(2,1)} async-done(((bf16[16,2,64512]{2,1,0:T(2,128)(2,1)}), bf16[16,2,64512]{2,1,0:T(2,128)(2,1)}, u32[]{:S(2)}, u32[]{:S(2)}) %all-to-all-start.3) | async-done | bytes 4128800 | tf_op jit(solution)/shard_map/all_to_all | solution.py:94
  448.3 12.2 %reshape.145 = bf16[16,1,129024]{2,1,0:T(2,128)(2,1)} reshape(bf16[16,2,64512]{2,1,0:T(2,128)(2,1)} %all-to-all-done.3) | data formatting | bytes 8257536
  460.5 26.1 %reduce.4 = bf16[16,129024]{1,0:T(8,128)(2,1)} reduce(bf16[16,1,129024]{2,1,0:T(2,128)(2,1)} %reshape.145, bf16[]{:T(256)} %constant.41), dimensions={1}, to_apply=%all_to_all.31.reduce_sub_computation | reduce | bytes 8257538 | tf_op jit(solution)/shard_map/all_to_all | solution.py:94
  486.6 9.1 %reshape.104 = bf16[576,3584]{1,0:T(8,128)(2,1)} reshape(bf16[16,129024]{1,0:T(8,128)(2,1)} %reduce.4) | data formatting | bytes 8257536 | tf_op jit(solution)/shard_map/reshape | solution.py:102
  495.7 3.8 convolution_convert_fusion.4
  502.5 25.9 %reduce-scatter.3.cloned.1.call-done = bf16[64,1792]{1,0:T(8,128)(2,1)} async-done(((bf16[64,3584]{1,0:T(8,128)(2,1)}), bf16[64,1792]{1,0:T(8,128)(2,1)}) %reduce-scatter.3.cloned.1.call-update) | async-done | bytes 229392 | tf_op jit(solution)/shard_map/reduce_scatter | solution.py:104
  (57 shorter events, 29.5 us)
Async XLA Ops:
  7.2 18.9 %copy-start = (bf16[64,3584]{1,0:T(8,128)(2,1)S(1)}, bf16[64,3584]{1,0:T(8,128)(2,1)}, u32[]{:S(2)}) copy-start(bf16[64,3584]{1,0:T(8,128)(2,1)} %param.8) | copy-start | bytes 1376260
  18.6 52.6 %all-to-all-start = ((bf16[16,1,36]{2,1,0:T(2,128)(2,1)}), bf16[16,1,36]{2,1,0:T(2,128)(2,1)S(1)}, u32[]{:S(2)}, u32[]{:S(2)}) async-start(bf16[16,1,36]{2,1,0:T(2,128)(2,1)} %all_to_all.32), calls=%async_computation | async-start | bytes 16384 | tf_op jit(solution)/shard_map/all_to_all | solution.py:51
  71.2 6.7 %copy-start.4 = (bf16[64,3584]{1,0:T(8,128)(2,1)S(1)}, bf16[64,3584]{1,0:T(8,128)(2,1)}, u32[]{:S(2)}) copy-start(bf16[64,3584]{1,0:T(8,128)(2,1)} %param.9) | copy-start | bytes 1376260
  71.2 83.1 %all-to-all-start.2 = ((bf16[16,2,64512]{2,1,0:T(2,128)(2,1)}), bf16[16,2,64512]{2,1,0:T(2,128)(2,1)}, u32[]{:S(2)}, u32[]{:S(2)}) async-start(bf16[16,2,64512]{2,1,0:T(2,128)(2,1)} %reshape.140), calls=%async_computation.2 | async-start | bytes 8257536 | tf_op jit(solution)/shard_map/all_to_all | solution.py:49
  154.2 96.0 %all-to-all-start.1 = ((bf16[16,2,64512]{2,1,0:T(2,128)(2,1)}), bf16[16,2,64512]{2,1,0:T(2,128)(2,1)}, u32[]{:S(2)}, u32[]{:S(2)}) async-start(bf16[16,2,64512]{2,1,0:T(2,128)(2,1)} %reshape.142), calls=%async_computation.1 | async-start | bytes 8257536 | tf_op jit(solution)/shard_map/all_to_all | solution.py:50
  221.3 5.7 %copy-start.2 = (bf16[576,3584]{1,0:T(8,128)(2,1)S(1)}, bf16[576,3584]{1,0:T(8,128)(2,1)}, u32[]{:S(2)}) copy-start(bf16[576,3584]{1,0:T(8,128)(2,1)} %reshape.103) | copy-start | bytes 12386308
  221.3 5.7 %copy-start.6 = (bf16[1,3584,512]{2,1,0:T(8,128)(2,1)S(1)}, bf16[1,3584,512]{2,1,0:T(8,128)(2,1)}, u32[]{:S(2)}) copy-start(bf16[1,3584,512]{2,1,0:T(8,128)(2,1)} %param.13) | copy-start | bytes 11010052
  227.0 70.7 %copy-start.8 = (f32[576,512]{1,0:T(8,128)}, f32[576,512]{1,0:T(8,128)S(1)}, u32[]{:S(2)}) copy-start(f32[576,512]{1,0:T(8,128)S(1)} %fusion.2) | copy-start | bytes 3538948
  297.7 6.4 %copy-start.5 = (bf16[1,3584,512]{2,1,0:T(8,128)(2,1)S(1)}, bf16[1,3584,512]{2,1,0:T(8,128)(2,1)}, u32[]{:S(2)}) copy-start(bf16[1,3584,512]{2,1,0:T(8,128)(2,1)} %param.12) | copy-start | bytes 11010052
  304.1 2.4 copy-start.7
  352.4 19.6 %copy-start.3 = (bf16[1,512,128]{2,1,0:T(8,128)(2,1)S(1)}, bf16[1,512,128]{2,1,0:T(8,128)(2,1)}, u32[]{:S(2)}) copy-start(bf16[1,512,128]{2,1,0:T(8,128)(2,1)} %param.15) | copy-start | bytes 393220
  352.4 96.0 %all-to-all-start.3 = ((bf16[16,2,64512]{2,1,0:T(2,128)(2,1)}), bf16[16,2,64512]{2,1,0:T(2,128)(2,1)}, u32[]{:S(2)}, u32[]{:S(2)}) async-start(bf16[16,2,64512]{2,1,0:T(2,128)(2,1)} %reshape.144), calls=%async_computation.3 | async-start | bytes 8257536 | tf_op jit(solution)/shard_map/all_to_all | solution.py:94
  371.9 127.6 %reduce-scatter.5.cloned.1.call-start = ((), (), s32[]{:S(2)}) async-start(), calls=%async_computation.7 | async-start | bytes 4128768 | tf_op jit(solution)/shard_map/reduce_scatter | solution.py:87
  382.4 145.9 %reduce-scatter.3.cloned.1.call-start = ((), (), s32[]{:S(2)}) async-start(), calls=%async_computation.6 | async-start | bytes 688128 | tf_op jit(solution)/shard_map/reduce_scatter | solution.py:104
  486.6 41.7 %copy-start.1 = (bf16[64,3584]{1,0:T(8,128)(2,1)S(1)}, bf16[64,3584]{1,0:T(8,128)(2,1)}, u32[]{:S(2)}) copy-start(bf16[64,3584]{1,0:T(8,128)(2,1)} %param.8) | copy-start | bytes 1376260
Sparse Core Ops, SparseCore 0:
  382.6 40.3 reduce-scatter.4
  499.7 28.6 reduce-scatter.2
where the time goes:
time: 544 us; the launch traced here: 536 us
  other arithmetic  162 us (30%)
  waiting for transfers between devices  144 us (26%)
  local copies, waits for them, and re-layouts  121 us (22%)
  starting transfers between devices  53.3 us (10%)
  matrix products  41.2 us (8%)
  between operations  14.7 us (3%)
    all_to_all x1, waiting for transfers between devices, on_device(): lax.all_to_all(part_rows.reshape(expert_count, capacity * model_width), '...  65.8 us
    unnamed x27, local copies, waits for them, and re-layouts  61 us
    all_to_all x2, other arithmetic, on_device(): lax.all_to_all(part_rows.reshape(expert_count, capacity * model_width), '...  52.9 us
    all_to_all x2, other arithmetic, on_device(): lax.all_to_all(to_slots(saved_inputs), 'expert', split_axis=0, concat_axi...  52.8 us
    all_to_all x2, other arithmetic, on_device(): lax.all_to_all(to_slots(output_grad), 'expert', split_axis=0, concat_axis...  52.8 us
    all_to_all x1, waiting for transfers between devices, on_device(): lax.all_to_all(to_slots(saved_inputs), 'expert', split_axis=0, concat_axi...  31.9 us
    reduce_scatter x1, waiting for transfers between devices, on_device(): lax.psum_scatter(spread.astype(jnp.bfloat16), 'dp', scatter_dimension=1,...  25.9 us
    all_to_all x1, waiting for transfers between devices, on_device(): lax.all_to_all(to_slots(output_grad), 'expert', split_axis=0, concat_axis...  19.9 us
  transfers between devices with their start and end apart: 6, of which 4 were waited for; matrix products, arithmetic and copies ran while one was open for 36% of the time, Pallas kernels for 0%

commit v1 on v0

--- a/solution.py
+++ b/solution.py
@@ -2,6 +2,27 @@
 import jax.numpy as jnp
 from jax import lax
 from jax.sharding import PartitionSpec as P
+from jax.lax import axis_index, axis_size, ppermute
+
+
+def _launch_pipes(local_block, lane_axis):
+    view_out = axis_size(lane_axis)
+    spare = axis_index(lane_axis)
+    t1, then = (view_out, spare)
+    aux = local_block.shape[0] // t1
+    k_now = list(local_block.shape)
+    k_now[0] = aux
+    lower = k_now[0]
+    k_now[0] = lower * t1
+    main = jnp.zeros(k_now, local_block.dtype)
+    for src_i in range(t1):
+        value_now = lax.dynamic_slice_in_dim(local_block, (then ^ src_i) * aux, aux, axis=0)
+        if src_i:
+            local_out = range(t1)
+            b_now = list(map(lambda u: (u, u ^ src_i), local_out))
+            value_now = ppermute(value_now, lane_axis, b_now)
+        main = lax.dynamic_update_slice_in_dim(main, value_now, (then ^ src_i) * lower, axis=0)
+    return main
 
 
 def on_device(
@@ -46,7 +67,7 @@
         return picked.reshape(expert_count, capacity * source_rows.shape[1])
 
     recv_inputs, recv_grads, recv_gates = (
-        lax.all_to_all(to_slots(saved_inputs), "expert", split_axis=0, concat_axis=0, tiled=True),
+        _launch_pipes(to_slots(saved_inputs), "expert"),
         lax.all_to_all(to_slots(output_grad), "expert", split_axis=0, concat_axis=0, tiled=True),
         lax.all_to_all(gate_slots, "expert", split_axis=0, concat_axis=0, tiled=True),
     )

time: 544 us -> 762 us (1.40)
  local copies, waits for them, and re-layouts: 121 us -> 294 us
  waiting for transfers between devices: 144 us -> 234 us
  other arithmetic: 162 us -> 109 us
  starting transfers between devices: 53.3 us -> 61.4 us
    dynamic_update_slice x0 -> x16, local copies, waits for them, and re-layouts: none -> 165 us  [_launch_pipes(): lax.dynamic_update_slice_in_dim(main, value_now, (then ^ src_i) * lower,...]
    ppermute x0 -> x15, waiting for transfers between devices: none -> 142 us  [_launch_pipes(): value_now = ppermute(value_now, lane_axis, b_now)]
    all_to_all x2 -> x0, other arithmetic: 52.8 us -> none  [on_device(): lax.all_to_all(to_slots(saved_inputs), 'expert', split_axis=0, concat_axi...]
    ppermute x0 -> x15, starting transfers between devices: none -> 41.6 us  [_launch_pipes(): value_now = ppermute(value_now, lane_axis, b_now)]
    all_to_all x1 -> x0, waiting for transfers between devices: 31.9 us -> none  [on_device(): lax.all_to_all(to_slots(saved_inputs), 'expert', split_axis=0, concat_axi...]
    dynamic_slice x0 -> x1, local copies, waits for them, and re-layouts: none -> 22.1 us  [_launch_pipes(): lax.dynamic_slice_in_dim(local_block, (then ^ src_i) * aux, aux, axis=0)]
    all_to_all x1, waiting for transfers between devices: 19.9 us -> 0.01 us  [on_device(): lax.all_to_all(to_slots(output_grad), 'expert', split_axis=0, concat_axis...]
    unnamed x27 -> x61, local copies, waits for them, and re-layouts: 61 us -> 42.8 us
  transfers between devices with their start and end apart: 6 -> 20, of which waited for: 4 -> 9; matrix products, arithmetic and copies ran while one was open for 36% -> 43% of each run, Pallas kernels for 0% -> 0%
where the time goes in v1:
time: 762 us; the launch traced here: 754 us
  local copies, waits for them, and re-layouts  294 us (39%)
  waiting for transfers between devices  234 us (31%)
  other arithmetic  109 us (14%)
  starting transfers between devices  61.4 us (8%)
  matrix products  41.1 us (5%)
  between operations  14.6 us (2%)
    dynamic_update_slice x16, local copies, waits for them, and re-layouts, _launch_pipes(): lax.dynamic_update_slice_in_dim(main, value_now, (then ^ src_i) * lower,...  165 us
    ppermute x15, waiting for transfers between devices, _launch_pipes(): value_now = ppermute(value_now, lane_axis, b_now)  142 us
    all_to_all x1, waiting for transfers between devices, on_device(): lax.all_to_all(part_rows.reshape(expert_count, capacity * model_width), '...  65.7 us
    all_to_all x2, other arithmetic, on_device(): lax.all_to_all(to_slots(output_grad), 'expert', split_axis=0, concat_axis...  52.8 us
    all_to_all x2, other arithmetic, on_device(): lax.all_to_all(part_rows.reshape(expert_count, capacity * model_width), '...  52.8 us
    unnamed x61, local copies, waits for them, and re-layouts  42.8 us
    ppermute x15, starting transfers between devices, _launch_pipes(): value_now = ppermute(value_now, lane_axis, b_now)  41.6 us
    reduce_scatter x1, waiting for transfers between devices, on_device(): lax.psum_scatter(spread.astype(jnp.bfloat16), 'dp', scatter_dimension=1,...  25.9 us
  transfers between devices with their start and end apart: 20, of which 9 were waited for; matrix products, arithmetic and copies ran while one was open for 43% of the time, Pallas kernels for 0%

profile of v1, /device:TPU:0, one launch (start us, length us, event | category | flops | bytes accessed | tf_op | source)
XLA Modules:
  0.0 753.8 jit_solution(6068990573552911849)
XLA Ops:
  50.7 26.7 %reduce.8 = bf16[16,129024]{1,0:T(8,128)(2,1)} reduce(bf16[16,1,129024]{2,1,0:T(2,128)(2,1)} %all_to_all.25, bf16[]{:T(256)} %broadcast.89), dimensions={1}, to_apply=%all_to_all.25.reduce_sub_computation | reduce | bytes 8257538 | tf_op jit(solution)/shard_map/all_to_all | solution.py:71
  90.9 22.1 %constant_dynamic-slice_fusion = (bf16[1,129024]{1,0:T(2,128)(2,1)S(1)}, bf16[1,129024]{1,0:T(2,128)(2,1)S(1)}, bf16[1,129024]{1,0:T(2,128)(2,1)S(1)}, bf16[1,12...) fusion(bf16[16,129024]{1,0:T(8,128)(2,1)} %reshape.101, ...), kind=kLoop, calls=%fused_computation.62 | loop fusion | bytes 8257600 | tf_op jit(solution)/shard_map/dynamic_slice | solution.py:19
  119.6 16.6 %collective-permute-done.1 = bf16[1,129024]{1,0:T(2,128)(2,1)S(1)} collective-permute-done((bf16[1,129024]{1,0:T(2,128)(2,1)S(1)}, bf16[1,129024]{1,0:T(2,128)(2,1)S(1)}, u32[]{:S(2)}, u32[]{:S(2)}) %collective-permute-start.1) | collective-permute-done | bytes 258080 | tf_op jit(solution)/shard_map/ppermute | solution.py:23
  136.3 18.6 %collective-permute-done.2 = bf16[1,129024]{1,0:T(2,128)(2,1)S(1)} collective-permute-done((bf16[1,129024]{1,0:T(2,128)(2,1)S(1)}, bf16[1,129024]{1,0:T(2,128)(2,1)S(1)}, u32[]{:S(2)}, u32[]{:S(2)}) %collective-permute-start.2) | collective-permute-done | bytes 258080 | tf_op jit(solution)/shard_map/ppermute | solution.py:23
  154.9 14.9 %collective-permute-done.3 = bf16[1,129024]{1,0:T(2,128)(2,1)S(1)} collective-permute-done((bf16[1,129024]{1,0:T(2,128)(2,1)S(1)}, bf16[1,129024]{1,0:T(2,128)(2,1)S(1)}, u32[]{:S(2)}, u32[]{:S(2)}) %collective-permute-start.3) | collective-permute-done | bytes 258080 | tf_op jit(solution)/shard_map/ppermute | solution.py:23
  181.9 25.0 %collective-permute-start.9 = (bf16[1,129024]{1,0:T(2,128)(2,1)S(1)}, bf16[1,129024]{1,0:T(2,128)(2,1)S(1)}, u32[]{:S(2)}, u32[]{:S(2)}) collective-permute-start(bf16[1,129024]{1,0:T(2,128)(2,1)S(1)} %get-tuple-element.17), channel_id=1, source_target_pairs={{0,10},{1,11},{2,8},{3,9},{4,14},{5,15},{6,12},{7,13},{8,2},{9,3},... | collective-permute-start | bytes 774152 | tf_op jit(solution)/shard_map/ppermute | solution.py:23
  207.0 11.4 %collective-permute-done.5 = bf16[1,129024]{1,0:T(2,128)(2,1)S(1)} collective-permute-done((bf16[1,129024]{1,0:T(2,128)(2,1)S(1)}, bf16[1,129024]{1,0:T(2,128)(2,1)S(1)}, u32[]{:S(2)}, u32[]{:S(2)}) %collective-permute-start.5) | collective-permute-done | bytes 258080 | tf_op jit(solution)/shard_map/ppermute | solution.py:23
  218.4 9.9 %collective-permute-done.6 = bf16[1,129024]{1,0:T(2,128)(2,1)S(1)} collective-permute-done((bf16[1,129024]{1,0:T(2,128)(2,1)S(1)}, bf16[1,129024]{1,0:T(2,128)(2,1)S(1)}, u32[]{:S(2)}, u32[]{:S(2)}) %collective-permute-start.6) | collective-permute-done | bytes 258080 | tf_op jit(solution)/shard_map/ppermute | solution.py:23
  234.3 61.9 %collective-permute-done.9 = bf16[1,129024]{1,0:T(2,128)(2,1)S(1)} collective-permute-done((bf16[1,129024]{1,0:T(2,128)(2,1)S(1)}, bf16[1,129024]{1,0:T(2,128)(2,1)S(1)}, u32[]{:S(2)}, u32[]{:S(2)}) %collective-permute-start.9) | collective-permute-done | bytes 258080 | tf_op jit(solution)/shard_map/ppermute | solution.py:23
  299.2 10.3 %dynamic_update_slice.48 = bf16[16,129024]{1,0:T(8,128)(2,1)} dynamic-update-slice(bf16[16,129024]{1,0:T(8,128)(2,1)} %broadcast_in_dim.17, bf16[1,129024]{1,0:T(2,128)(2,1)S(1)} %get-tuple-element.27, s32[]{:T(128)S(6)} %select_n.90, s32[]{:T(128)} %constant.27.clone.1) | dynamic-update-slice | bytes 516100 | tf_op jit(solution)/shard_map/dynamic_update_slice | solution.py:24
  309.6 10.4 %dynamic_update_slice.49 = bf16[16,129024]{1,0:T(8,128)(2,1)} dynamic-update-slice(bf16[16,129024]{1,0:T(8,128)(2,1)} %dynamic_update_slice.48, bf16[1,129024]{1,0:T(2,128)(2,1)} %copy-done.4, s32[]{:T(128)S(6)} %select_n.91, s32[]{:T(128)} %constant.27.clone.1) | dynamic-update-slice | bytes 516100 | tf_op jit(solution)/shard_map/dynamic_update_slice | solution.py:24
  320.0 10.3 %dynamic_update_slice.50 = bf16[16,129024]{1,0:T(8,128)(2,1)} dynamic-update-slice(bf16[16,129024]{1,0:T(8,128)(2,1)} %dynamic_update_slice.49, bf16[1,129024]{1,0:T(2,128)(2,1)} %copy-done.5, s32[]{:T(128)S(6)} %select_n.92, s32[]{:T(128)} %constant.27.clone.1) | dynamic-update-slice | bytes 516100 | tf_op jit(solution)/shard_map/dynamic_update_slice | solution.py:24
  330.4 10.3 %dynamic_update_slice.51 = bf16[16,129024]{1,0:T(8,128)(2,1)} dynamic-update-slice(bf16[16,129024]{1,0:T(8,128)(2,1)} %dynamic_update_slice.50, bf16[1,129024]{1,0:T(2,128)(2,1)} %copy-done.6, s32[]{:T(128)S(6)} %select_n.93, s32[]{:T(128)} %constant.27.clone.1) | dynamic-update-slice | bytes 516100 | tf_op jit(solution)/shard_map/dynamic_update_slice | solution.py:24
  340.7 10.3 %dynamic_update_slice.52 = bf16[16,129024]{1,0:T(8,128)(2,1)} dynamic-update-slice(bf16[16,129024]{1,0:T(8,128)(2,1)} %dynamic_update_slice.51, bf16[1,129024]{1,0:T(2,128)(2,1)} %copy-done.7, s32[]{:T(128)S(6)} %select_n.94, s32[]{:T(128)} %constant.27.clone.1) | dynamic-update-slice | bytes 516100 | tf_op jit(solution)/shard_map/dynamic_update_slice | solution.py:24
  351.0 10.3 %dynamic_update_slice.53 = bf16[16,129024]{1,0:T(8,128)(2,1)} dynamic-update-slice(bf16[16,129024]{1,0:T(8,128)(2,1)} %dynamic_update_slice.52, bf16[1,129024]{1,0:T(2,128)(2,1)S(1)} %copy-done.9, s32[]{:T(128)S(6)} %select_n.95, s32[]{:T(128)} %constant.27.clone.1) | dynamic-update-slice | bytes 516100 | tf_op jit(solution)/shard_map/dynamic_update_slice | solution.py:24
  361.3 10.4 %dynamic_update_slice.54 = bf16[16,129024]{1,0:T(8,128)(2,1)} dynamic-update-slice(bf16[16,129024]{1,0:T(8,128)(2,1)} %dynamic_update_slice.53, bf16[1,129024]{1,0:T(2,128)(2,1)} %copy-done.10, s32[]{:T(128)S(6)} %select_n.96, s32[]{:T(128)} %constant.27.clone.1) | dynamic-update-slice | bytes 516100 | tf_op jit(solution)/shard_map/dynamic_update_slice | solution.py:24
  371.7 10.3 %dynamic_update_slice.55 = bf16[16,129024]{1,0:T(8,128)(2,1)} dynamic-update-slice(bf16[16,129024]{1,0:T(8,128)(2,1)} %dynamic_update_slice.54, bf16[1,129024]{1,0:T(2,128)(2,1)} %copy-done.11, s32[]{:T(128)S(6)} %select_n.97, s32[]{:T(128)} %constant.27.clone.1) | dynamic-update-slice | bytes 516100 | tf_op jit(solution)/shard_map/dynamic_update_slice | solution.py:24
  382.1 10.3 %dynamic_update_slice.56 = bf16[16,129024]{1,0:T(8,128)(2,1)} dynamic-update-slice(bf16[16,129024]{1,0:T(8,128)(2,1)} %dynamic_update_slice.55, bf16[1,129024]{1,0:T(2,128)(2,1)} %copy-done.12, s32[]{:T(128)S(6)} %select_n.98, s32[]{:T(128)} %constant.27.clone.1) | dynamic-update-slice | bytes 516100 | tf_op jit(solution)/shard_map/dynamic_update_slice | solution.py:24
  392.4 10.3 %dynamic_update_slice.57 = bf16[16,129024]{1,0:T(8,128)(2,1)} dynamic-update-slice(bf16[16,129024]{1,0:T(8,128)(2,1)} %dynamic_update_slice.56, bf16[1,129024]{1,0:T(2,128)(2,1)} %copy-done.13, s32[]{:T(128)S(6)} %select_n.99, s32[]{:T(128)} %constant.27.clone.1) | dynamic-update-slice | bytes 516100 | tf_op jit(solution)/shard_map/dynamic_update_slice | solution.py:24
  402.7 10.3 %dynamic_update_slice.58 = bf16[16,129024]{1,0:T(8,128)(2,1)} dynamic-update-slice(bf16[16,129024]{1,0:T(8,128)(2,1)} %dynamic_update_slice.57, bf16[1,129024]{1,0:T(2,128)(2,1)S(1)} %copy-done.15, s32[]{:T(128)S(6)} %select_n.100, s32[]{:T(128)} %constant.27.clone.1) | dynamic-update-slice | bytes 516100 | tf_op jit(solution)/shard_map/dynamic_update_slice | solution.py:24
  413.0 10.3 %dynamic_update_slice.59 = bf16[16,129024]{1,0:T(8,128)(2,1)} dynamic-update-slice(bf16[16,129024]{1,0:T(8,128)(2,1)} %dynamic_update_slice.58, bf16[1,129024]{1,0:T(2,128)(2,1)} %collective-permute-done.10, s32[]{:T(128)S(6)} %select_n.101, s32[]{:T(128)} %constant.27.clone.1) | dynamic-update-slice | bytes 516100 | tf_op jit(solution)/shard_map/dynamic_update_slice | solution.py:24
  423.3 10.3 %dynamic_update_slice.60 = bf16[16,129024]{1,0:T(8,128)(2,1)} dynamic-update-slice(bf16[16,129024]{1,0:T(8,128)(2,1)} %dynamic_update_slice.59, bf16[1,129024]{1,0:T(2,128)(2,1)} %collective-permute-done.11, s32[]{:T(128)S(6)} %select_n.102, s32[]{:T(128)} %constant.27.clone.1) | dynamic-update-slice | bytes 516100 | tf_op jit(solution)/shard_map/dynamic_update_slice | solution.py:24
  433.6 10.3 %dynamic_update_slice.61 = bf16[16,129024]{1,0:T(8,128)(2,1)} dynamic-update-slice(bf16[16,129024]{1,0:T(8,128)(2,1)} %dynamic_update_slice.60, bf16[1,129024]{1,0:T(2,128)(2,1)} %collective-permute-done.12, s32[]{:T(128)S(6)} %select_n.103, s32[]{:T(128)} %constant.27.clone.1) | dynamic-update-slice | bytes 516100 | tf_op jit(solution)/shard_map/dynamic_update_slice | solution.py:24
  444.0 10.3 %dynamic_update_slice.62 = bf16[16,129024]{1,0:T(8,128)(2,1)} dynamic-update-slice(bf16[16,129024]{1,0:T(8,128)(2,1)} %dynamic_update_slice.61, bf16[1,129024]{1,0:T(2,128)(2,1)} %collective-permute-done.13, s32[]{:T(128)S(6)} %select_n.104, s32[]{:T(128)} %constant.27.clone.1) | dynamic-update-slice | bytes 516100 | tf_op jit(solution)/shard_map/dynamic_update_slice | solution.py:24
  454.3 10.3 %dynamic_update_slice.63 = bf16[16,129024]{1,0:T(8,128)(2,1)} dynamic-update-slice(bf16[16,129024]{1,0:T(8,128)(2,1)} %dynamic_update_slice.62, bf16[1,129024]{1,0:T(2,128)(2,1)} %collective-permute-done.14, s32[]{:T(128)S(6)} %select_n.105, s32[]{:T(128)} %constant.27.clone.1) | dynamic-update-slice | bytes 516100 | tf_op jit(solution)/shard_map/dynamic_update_slice | solution.py:24
  482.9 12.2 %reshape.139 = bf16[16,1,129024]{2,1,0:T(2,128)(2,1)} reshape(bf16[16,2,64512]{2,1,0:T(2,128)(2,1)} %all-to-all-done.1) | data formatting | bytes 8257536
  495.1 26.1 %reduce.2 = bf16[16,129024]{1,0:T(8,128)(2,1)} reduce(bf16[16,1,129024]{2,1,0:T(2,128)(2,1)} %reshape.139, bf16[]{:T(256)} %constant.74), dimensions={1}, to_apply=%all_to_all.21.reduce_sub_computation | reduce | bytes 8257538 | tf_op jit(solution)/shard_map/all_to_all | solution.py:71
  551.8 26.7 %reduce.9 = bf16[16,129024]{1,0:T(8,128)(2,1)} reduce(bf16[16,1,129024]{2,1,0:T(2,128)(2,1)} %all_to_all.26, bf16[]{:T(256)} %broadcast.89), dimensions={1}, to_apply=%all_to_all.26.reduce_sub_computation | reduce | bytes 8257538 | tf_op jit(solution)/shard_map/all_to_all | solution.py:115
  601.1 65.7 %all-to-all-done.2 = bf16[16,2,64512]{2,1,0:T(2,128)(2,1)} async-done(((bf16[16,2,64512]{2,1,0:T(2,128)(2,1)}), bf16[16,2,64512]{2,1,0:T(2,128)(2,1)}, u32[]{:S(2)}, u32[]{:S(2)}) %all-to-all-start.2) | async-done | bytes 4128800 | tf_op jit(solution)/shard_map/all_to_all | solution.py:115
  666.7 12.2 %reshape.141 = bf16[16,1,129024]{2,1,0:T(2,128)(2,1)} reshape(bf16[16,2,64512]{2,1,0:T(2,128)(2,1)} %all-to-all-done.2) | data formatting | bytes 8257536
  678.9 26.1 %reduce.3 = bf16[16,129024]{1,0:T(8,128)(2,1)} reduce(bf16[16,1,129024]{2,1,0:T(2,128)(2,1)} %reshape.141, bf16[]{:T(256)} %constant.74), dimensions={1}, to_apply=%all_to_all.23.reduce_sub_computation | reduce | bytes 8257538 | tf_op jit(solution)/shard_map/all_to_all | solution.py:115
  720.9 25.9 %reduce-scatter.3.cloned.1.call-done = bf16[64,1792]{1,0:T(8,128)(2,1)} async-done(((bf16[64,3584]{1,0:T(8,128)(2,1)}), bf16[64,1792]{1,0:T(8,128)(2,1)}) %reduce-scatter.3.cloned.1.call-update) | async-done | bytes 229392 | tf_op jit(solution)/shard_map/reduce_scatter | solution.py:125
  (135 shorter events, 172.0 us)
Async XLA Ops:
  18.7 65.3 %all-to-all-start = ((bf16[16,1,36]{2,1,0:T(2,128)(2,1)}), bf16[16,1,36]{2,1,0:T(2,128)(2,1)S(1)}, u32[]{:S(2)}, u32[]{:S(2)}) async-start(bf16[16,1,36]{2,1,0:T(2,128)(2,1)} %all_to_all.24), calls=%async_computation | async-start | bytes 16384 | tf_op jit(solution)/shard_map/all_to_all | solution.py:72
  84.6 398.3 %all-to-all-start.1 = ((bf16[16,2,64512]{2,1,0:T(2,128)(2,1)}), bf16[16,2,64512]{2,1,0:T(2,128)(2,1)}, u32[]{:S(2)}, u32[]{:S(2)}) async-start(bf16[16,2,64512]{2,1,0:T(2,128)(2,1)} %reshape.138), calls=%async_computation.1 | async-start | bytes 8257536 | tf_op jit(solution)/shard_map/all_to_all | solution.py:71
  113.0 196.5 %copy-start.22 = (bf16[16,1,36]{2,1,0:T(2,128)(2,1)S(1)}, bf16[16,1,36]{2,1,0:T(2,128)(2,1)}, u32[]{:S(2)}) copy-start(bf16[16,1,36]{2,1,0:T(2,128)(2,1)} %copy-done.21) | copy-start | bytes 3460
  113.0 4.1 collective-permute-start
  113.6 22.7 %collective-permute-start.1 = (bf16[1,129024]{1,0:T(2,128)(2,1)S(1)}, bf16[1,129024]{1,0:T(2,128)(2,1)S(1)}, u32[]{:S(2)}, u32[]{:S(2)}) collective-permute-start(bf16[1,129024]{1,0:T(2,128)(2,1)S(1)} %get-tuple-element.25), channel_id=1, source_target_pairs={{0,2},{1,3},{2,0},{3,1},{4,6},{5,7},{6,4},{7,5},{8,10},{9,11},{10,... | collective-permute-start | bytes 774152 | tf_op jit(solution)/shard_map/ppermute | solution.py:23
  115.2 39.7 %collective-permute-start.2 = (bf16[1,129024]{1,0:T(2,128)(2,1)S(1)}, bf16[1,129024]{1,0:T(2,128)(2,1)S(1)}, u32[]{:S(2)}, u32[]{:S(2)}) collective-permute-start(bf16[1,129024]{1,0:T(2,128)(2,1)S(1)} %get-tuple-element.24), channel_id=1, source_target_pairs={{0,3},{1,2},{2,1},{3,0},{4,7},{5,6},{6,5},{7,4},{8,11},{9,10},{10,... | collective-permute-start | bytes 774152 | tf_op jit(solution)/shard_map/ppermute | solution.py:23
  115.2 54.6 %collective-permute-start.3 = (bf16[1,129024]{1,0:T(2,128)(2,1)S(1)}, bf16[1,129024]{1,0:T(2,128)(2,1)S(1)}, u32[]{:S(2)}, u32[]{:S(2)}) collective-permute-start(bf16[1,129024]{1,0:T(2,128)(2,1)S(1)} %get-tuple-element.23), channel_id=1, source_target_pairs={{0,4},{1,5},{2,6},{3,7},{4,0},{5,1},{6,2},{7,3},{8,12},{9,13},{10,... | collective-permute-start | bytes 774152 | tf_op jit(solution)/shard_map/ppermute | solution.py:23
  117.0 64.9 %collective-permute-start.4 = (bf16[1,129024]{1,0:T(2,128)(2,1)S(1)}, bf16[1,129024]{1,0:T(2,128)(2,1)S(1)}, u32[]{:S(2)}, u32[]{:S(2)}) collective-permute-start(bf16[1,129024]{1,0:T(2,128)(2,1)S(1)} %get-tuple-element.22), channel_id=1, source_target_pairs={{0,5},{1,4},{2,7},{3,6},{4,1},{5,0},{6,3},{7,2},{8,13},{9,12},{10,... | collective-permute-start | bytes 774152 | tf_op jit(solution)/shard_map/ppermute | solution.py:23
  117.1 179.8 %copy-start.4 = (bf16[1,129024]{1,0:T(2,128)(2,1)}, bf16[1,129024]{1,0:T(2,128)(2,1)S(1)}, u32[]{:S(2)}) copy-start(bf16[1,129024]{1,0:T(2,128)(2,1)S(1)} %collective-permute-done) | copy-start | bytes 774148
  117.1 101.2 %collective-permute-start.5 = (bf16[1,129024]{1,0:T(2,128)(2,1)S(1)}, bf16[1,129024]{1,0:T(2,128)(2,1)S(1)}, u32[]{:S(2)}, u32[]{:S(2)}) collective-permute-start(bf16[1,129024]{1,0:T(2,128)(2,1)S(1)} %get-tuple-element.21), channel_id=1, source_target_pairs={{0,6},{1,7},{2,4},{3,5},{4,2},{5,3},{6,0},{7,1},{8,14},{9,15},{10,... | collective-permute-start | bytes 774152 | tf_op jit(solution)/shard_map/ppermute | solution.py:23
  136.3 160.6 %copy-start.5 = (bf16[1,129024]{1,0:T(2,128)(2,1)}, bf16[1,129024]{1,0:T(2,128)(2,1)S(1)}, u32[]{:S(2)}) copy-start(bf16[1,129024]{1,0:T(2,128)(2,1)S(1)} %collective-permute-done.1) | copy-start | bytes 774148
  136.3 92.0 %collective-permute-start.6 = (bf16[1,129024]{1,0:T(2,128)(2,1)S(1)}, bf16[1,129024]{1,0:T(2,128)(2,1)S(1)}, u32[]{:S(2)}, u32[]{:S(2)}) collective-permute-start(bf16[1,129024]{1,0:T(2,128)(2,1)S(1)} %get-tuple-element.20), channel_id=1, source_target_pairs={{0,7},{1,6},{2,5},{3,4},{4,3},{5,2},{6,1},{7,0},{8,15},{9,14},{10,... | collective-permute-start | bytes 774152 | tf_op jit(solution)/shard_map/ppermute | solution.py:23
  154.9 142.0 %copy-start.6 = (bf16[1,129024]{1,0:T(2,128)(2,1)}, bf16[1,129024]{1,0:T(2,128)(2,1)S(1)}, u32[]{:S(2)}) copy-start(bf16[1,129024]{1,0:T(2,128)(2,1)S(1)} %collective-permute-done.2) | copy-start | bytes 774148
  154.9 75.6 %collective-permute-start.7 = (bf16[1,129024]{1,0:T(2,128)(2,1)S(1)}, bf16[1,129024]{1,0:T(2,128)(2,1)S(1)}, u32[]{:S(2)}, u32[]{:S(2)}) collective-permute-start(bf16[1,129024]{1,0:T(2,128)(2,1)S(1)} %get-tuple-element.19), channel_id=1, source_target_pairs={{0,8},{1,9},{2,10},{3,11},{4,12},{5,13},{6,14},{7,15},{8,0},{9,1},... | collective-permute-start | bytes 774152 | tf_op jit(solution)/shard_map/ppermute | solution.py:23
  169.8 127.1 %copy-start.7 = (bf16[1,129024]{1,0:T(2,128)(2,1)}, bf16[1,129024]{1,0:T(2,128)(2,1)S(1)}, u32[]{:S(2)}) copy-start(bf16[1,129024]{1,0:T(2,128)(2,1)S(1)} %collective-permute-done.3) | copy-start | bytes 774148
  169.8 62.0 %collective-permute-start.8 = (bf16[1,129024]{1,0:T(2,128)(2,1)S(1)}, bf16[1,129024]{1,0:T(2,128)(2,1)S(1)}, u32[]{:S(2)}, u32[]{:S(2)}) collective-permute-start(bf16[1,129024]{1,0:T(2,128)(2,1)S(1)} %get-tuple-element.18), channel_id=1, source_target_pairs={{0,9},{1,8},{2,11},{3,10},{4,13},{5,12},{6,15},{7,14},{8,1},{9,0},... | collective-permute-start | bytes 774152 | tf_op jit(solution)/shard_map/ppermute | solution.py:23
  181.9 115.0 %copy-start.8 = (bf16[1,129024]{1,0:T(2,128)(2,1)}, bf16[1,129024]{1,0:T(2,128)(2,1)S(1)}, u32[]{:S(2)}) copy-start(bf16[1,129024]{1,0:T(2,128)(2,1)S(1)} %collective-permute-done.4) | copy-start | bytes 774148
  181.9 114.3 %collective-permute-start.9 = (bf16[1,129024]{1,0:T(2,128)(2,1)S(1)}, bf16[1,129024]{1,0:T(2,128)(2,1)S(1)}, u32[]{:S(2)}, u32[]{:S(2)}) collective-permute-start(bf16[1,129024]{1,0:T(2,128)(2,1)S(1)} %get-tuple-element.17), channel_id=1, source_target_pairs={{0,10},{1,11},{2,8},{3,9},{4,14},{5,15},{6,12},{7,13},{8,2},{9,3},... | collective-permute-start | bytes 774152 | tf_op jit(solution)/shard_map/ppermute | solution.py:23
  218.4 78.6 %copy-start.10 = (bf16[1,129024]{1,0:T(2,128)(2,1)}, bf16[1,129024]{1,0:T(2,128)(2,1)S(1)}, u32[]{:S(2)}) copy-start(bf16[1,129024]{1,0:T(2,128)(2,1)S(1)} %collective-permute-done.5) | copy-start | bytes 774148
  218.4 194.6 %collective-permute-start.10 = (bf16[1,129024]{1,0:T(2,128)(2,1)S(1)}, bf16[1,129024]{1,0:T(2,128)(2,1)}, u32[]{:S(2)}, u32[]{:S(2)}) collective-permute-start(bf16[1,129024]{1,0:T(2,128)(2,1)S(1)} %get-tuple-element.16), channel_id=1, source_target_pairs={{0,11},{1,10},{2,9},{3,8},{4,15},{5,14},{6,13},{7,12},{8,3},{9,2},... | collective-permute-start | bytes 774152 | tf_op jit(solution)/shard_map/ppermute | solution.py:23
  228.3 68.7 %copy-start.11 = (bf16[1,129024]{1,0:T(2,128)(2,1)}, bf16[1,129024]{1,0:T(2,128)(2,1)S(1)}, u32[]{:S(2)}) copy-start(bf16[1,129024]{1,0:T(2,128)(2,1)S(1)} %collective-permute-done.6) | copy-start | bytes 774148
  228.3 195.0 %collective-permute-start.11 = (bf16[1,129024]{1,0:T(2,128)(2,1)S(1)}, bf16[1,129024]{1,0:T(2,128)(2,1)}, u32[]{:S(2)}, u32[]{:S(2)}) collective-permute-start(bf16[1,129024]{1,0:T(2,128)(2,1)S(1)} %get-tuple-element.15), channel_id=1, source_target_pairs={{0,12},{1,13},{2,14},{3,15},{4,8},{5,9},{6,10},{7,11},{8,4},{9,5},... | collective-permute-start | bytes 774152 | tf_op jit(solution)/shard_map/ppermute | solution.py:23
  230.5 66.4 %copy-start.12 = (bf16[1,129024]{1,0:T(2,128)(2,1)}, bf16[1,129024]{1,0:T(2,128)(2,1)S(1)}, u32[]{:S(2)}) copy-start(bf16[1,129024]{1,0:T(2,128)(2,1)S(1)} %collective-permute-done.7) | copy-start | bytes 774148
  230.5 203.1 %collective-permute-start.12 = (bf16[1,129024]{1,0:T(2,128)(2,1)S(1)}, bf16[1,129024]{1,0:T(2,128)(2,1)}, u32[]{:S(2)}, u32[]{:S(2)}) collective-permute-start(bf16[1,129024]{1,0:T(2,128)(2,1)S(1)} %get-tuple-element.14), channel_id=1, source_target_pairs={{0,13},{1,12},{2,15},{3,14},{4,9},{5,8},{6,11},{7,10},{8,5},{9,4},... | collective-permute-start | bytes 774152 | tf_op jit(solution)/shard_map/ppermute | solution.py:23
  231.8 65.1 %copy-start.13 = (bf16[1,129024]{1,0:T(2,128)(2,1)}, bf16[1,129024]{1,0:T(2,128)(2,1)S(1)}, u32[]{:S(2)}) copy-start(bf16[1,129024]{1,0:T(2,128)(2,1)S(1)} %collective-permute-done.8) | copy-start | bytes 774148
  231.8 212.1 %collective-permute-start.13 = (bf16[1,129024]{1,0:T(2,128)(2,1)S(1)}, bf16[1,129024]{1,0:T(2,128)(2,1)}, u32[]{:S(2)}, u32[]{:S(2)}) collective-permute-start(bf16[1,129024]{1,0:T(2,128)(2,1)S(1)} %get-tuple-element.13), channel_id=1, source_target_pairs={{0,14},{1,15},{2,12},{3,13},{4,10},{5,11},{6,8},{7,9},{8,6},{9,7},... | collective-permute-start | bytes 774152 | tf_op jit(solution)/shard_map/ppermute | solution.py:23
  296.2 158.1 %collective-permute-start.14 = (bf16[1,129024]{1,0:T(2,128)(2,1)S(1)}, bf16[1,129024]{1,0:T(2,128)(2,1)}, u32[]{:S(2)}, u32[]{:S(2)}) collective-permute-start(bf16[1,129024]{1,0:T(2,128)(2,1)S(1)} %get-tuple-element.12), channel_id=1, source_target_pairs={{0,15},{1,14},{2,13},{3,12},{4,11},{5,10},{6,9},{7,8},{8,7},{9,6},... | collective-permute-start | bytes 774152 | tf_op jit(solution)/shard_map/ppermute | solution.py:23
  479.6 51.0 %copy-start.26 = (f32[576,512]{1,0:T(8,128)}, f32[576,512]{1,0:T(8,128)S(1)}, u32[]{:S(2)}) copy-start(f32[576,512]{1,0:T(8,128)S(1)} %fusion.2) | copy-start | bytes 3538948
  585.0 81.7 %all-to-all-start.2 = ((bf16[16,2,64512]{2,1,0:T(2,128)(2,1)}), bf16[16,2,64512]{2,1,0:T(2,128)(2,1)}, u32[]{:S(2)}, u32[]{:S(2)}) async-start(bf16[16,2,64512]{2,1,0:T(2,128)(2,1)} %reshape.140), calls=%async_computation.2 | async-start | bytes 8257536 | tf_op jit(solution)/shard_map/all_to_all | solution.py:115
  590.3 127.7 %reduce-scatter.5.cloned.1.call-start = ((), (), s32[]{:S(2)}) async-start(), calls=%async_computation.6 | async-start | bytes 4128768 | tf_op jit(solution)/shard_map/reduce_scatter | solution.py:108
  601.0 145.8 %reduce-scatter.3.cloned.1.call-start = ((), (), s32[]{:S(2)}) async-start(), calls=%async_computation.5 | async-start | bytes 688128 | tf_op jit(solution)/shard_map/reduce_scatter | solution.py:125
  705.0 41.8 %copy-start.1 = (bf16[64,3584]{1,0:T(8,128)(2,1)S(1)}, bf16[64,3584]{1,0:T(8,128)(2,1)}, u32[]{:S(2)}) copy-start(bf16[64,3584]{1,0:T(8,128)(2,1)} %param.8) | copy-start | bytes 1376260
  (15 other events, 191.7 us)
Sparse Core Ops, SparseCore 0:
  601.1 40.3 reduce-scatter.4
  718.1 28.6 reduce-scatter.2
